TPU v7x, 32 devices: a whole 2x2x4 slice. The times are simulated.
32 devices in a mesh: batch: 8 (over z, y), tensor: 2 (over x), section: 2 (over core).
Axes of the slice: x: 2, y: 2, z: 4, core: 2. Of those that a mesh axis runs over, the one named last changes fastest.
Arguments:
- prefill_cache: bfloat16 [2, 32, 2, 4, 256, 128], P('section', ('batch', 'tensor')), may hold values from -5 to 5
- lengths: int32 [32], P('batch'), may hold values from 1 to 256, as said below
- page_table: int32 [32, 1], P('batch'), may hold values from -1 to 3, as said below
- holder: int32 [8, 4], replicated, may hold values from 0 to 7, as said below
- queries: bfloat16 [32, 2, 4, 32, 128], P(('batch', 'section'), None, None, 'tensor'), may hold values from -120 to 120
- new_kv: bfloat16 [32, 2, 4, 2, 4, 128], P(('batch', 'section'), None, None, None, 'tensor'), may hold values from -5 to 5
Outputs:
- attended: bfloat16 [32, 2, 4, 32, 128], P(('batch', 'section'), None, None, 'tensor')
- decode_pool: bfloat16 [2, 32, 2, 4, 256, 128], P('section', 'batch', None, 'tensor')
Inputs may be any that keep to these rules, and one draw needn't show every extreme that they name: Request r's prompt has lengths[r] tokens, held in ceil(lengths[r] / 256) pages. `page_table`: row r names in its first ceil(lengths[r] / 256) columns the pool positions (0 to 3) of the request's pages in order, and -1 after; a position is named at most once among the 4 requests of one batch index; some batch index uses all 4 positions. holder[b, q] = b XOR key_q (bitwise exclusive or of the binary digits), where key_0 to key_7 are distinct numbers of 0 to 7; so each column is a permutation of the batch indices and each row names distinct ones.
All inputs are finite; a program needn't handle non-finite values.
Results may differ from a plain program's by a relative error of at most 0.0038.
Values may be sent and summed in bfloat16 or wider, within the bound.
A program may use at most 64 MiB of HBM per device.

v0:
```python
import functools
import math

import jax
import jax.numpy as jnp
from jax import lax
from jax.experimental import pallas as pl
from jax.experimental.pallas import tpu as pltpu
from jax.sharding import PartitionSpec as P

MASKED = -1e30


def shortened(shard):
    return jax.tree.map(lambda a: a.astype(jnp.bfloat16) if a.dtype == jnp.float32 else a, shard)


def partner_2(value, axis, bit):
    mask = 2**bit
    pairs = [(source, source ^ mask) for source in range(lax.axis_size(axis))]
    return lax.ppermute(value, axis, pairs)


def pick_where(take, partner, current):
    return tuple(
        (
            jnp.where(take.reshape((-1,) + (1,) * (own.ndim - 1)), other, own)
            for other, own in zip(partner, current)
        )
    )


def sends_by_key(batch_count, positions):
    return batch_count % 4 == 0 and batch_count <= 2 * positions


def exclusive_or(value, mask, count):
    total = 0
    bit = 1
    while bit < count:
        total = total + lax.rem(value // bit + mask // bit % 2, 2) * bit
        bit *= 2
    return total


MESH = pl.DeviceIdType.MESH


def rows_of(heads):
    wide = heads.astype(jnp.float32).reshape(-1, heads.shape[-1])
    return wide.astype(jnp.bfloat16)


def scores_of(query_rows, key_rows):
    product = lax.dot_general(
        query_rows, key_rows, (((1,), (1,)), ((), ())), preferred_element_type=jnp.float32
    )
    return product * (1.0 / math.sqrt(query_rows.shape[-1]))


def softmax_parts(scores, mask):
    peak = jnp.max(jnp.where(mask, scores, MASKED), axis=-1, keepdims=True)
    weights = jnp.where(mask, jnp.exp(scores - peak), 0.0).astype(jnp.bfloat16)
    total = jnp.sum(weights.astype(jnp.float32), axis=-1, keepdims=True)
    return peak, weights, total


def kernel(
    tensors, sections, batches, by_key,
    lengths, page_table, keys, cache, queries, new_rows,
    *rest,
):
    positions = keys.shape[0]
    outs = 1 if by_key else positions
    slots_out = rest[:outs]
    attended, rest = rest[outs], rest[outs + 1 :]
    kv_local = cache.shape[3] // tensors
    chunks = [(entry, place) for entry in range(2) for place in range(kv_local)]
    pages, rest = rest[: len(chunks)], rest[len(chunks) :]
    (layer_queries, page_out, page_peak, page_sum, new_out, new_peak, new_sum,
     outgoing, merged, load_sem, page_send, page_recv, query_sems, part_sems) = rest[:14]
    if by_key:
        leaving, passing, key_send, key_recv, pass_send, pass_recv, on_send = rest[14:21]
        landing = rest[21:]
    tensor, section = lax.axis_index("tensor"), lax.axis_index("section")
    batch = lax.axis_index("batch")
    local_pages = cache.shape[1]
    page_len, head = cache.shape[4], cache.shape[5]
    owned, layers, steps, heads = queries.shape[:4]
    requests = owned * sections
    columns_of = page_table.shape[0] // requests
    group = heads // kv_local
    rows = steps * heads

    quarter = max(batches // 4, 1)
    stretch, offset = batch // quarter, lax.rem(batch, quarter)
    up = lax.rem(stretch + 1, 4) * quarter + offset
    down = lax.rem(stretch + 3, 4) * quarter + offset

    barrier = pltpu.get_barrier_semaphore()
    greeted = 0
    for ahead in range(1, tensors):
        other = lax.rem(tensor + ahead, tensors)
        pl.semaphore_signal(barrier, inc=1, device_id={"tensor": other}, device_id_type=MESH)
        greeted += 1
    for ahead in range(1, sections):
        other = lax.rem(section + ahead, sections)
        pl.semaphore_signal(barrier, inc=1, device_id={"section": other}, device_id_type=MESH)
        greeted += 1
    if by_key:
        for key in range(1, batches):
            other = exclusive_or(batch, key, batches)
            pl.semaphore_signal(barrier, inc=1, device_id={"batch": other}, device_id_type=MESH)
            greeted += 1

    own_pages = []
    for chunk, (entry, place) in enumerate(chunks):
        copy = pltpu.make_async_copy(
            cache.at[0, :, entry, tensor * kv_local + place],
            pages[chunk].at[pl.ds(tensor * local_pages, local_pages)],
            load_sem.at[1 + chunk],
        )
        copy.start()
        own_pages.append(copy)
    own_queries = pltpu.make_async_copy(
        queries.at[:, section], layer_queries.at[pl.ds(section * owned, owned)], load_sem.at[0]
    )
    own_queries.start()
    pl.semaphore_wait(barrier, greeted)

    page_copies = []
    for chunk, (entry, place) in enumerate(chunks):
        copies = []
        for page in range(local_pages):
            for ahead in range(1, tensors):
                other = lax.rem(tensor + ahead, tensors)
                copy = pltpu.make_async_remote_copy(
                    src_ref=cache.at[0, page, entry, other * kv_local + place],
                    dst_ref=pages[chunk].at[tensor * local_pages + page],
                    send_sem=page_send.at[ahead - 1, page, chunk],
                    recv_sem=page_recv.at[ahead - 1, page, chunk],
                    device_id={"tensor": other},
                    device_id_type=MESH,
                )
                copy.start()
                copies.append(copy)
        page_copies.append(copies)
    query_copies = []
    for ahead in range(1, sections):
        other = lax.rem(section + ahead, sections)
        copy = pltpu.make_async_remote_copy(
            src_ref=queries.at[:, other],
            dst_ref=layer_queries.at[pl.ds(section * owned, owned)],
            send_sem=query_sems.at[0, ahead - 1],
            recv_sem=query_sems.at[1, ahead - 1],
            device_id={"section": other},
            device_id_type=MESH,
        )
        copy.start()
        query_copies.append(copy)

    request_of, used, live = [], [], []
    for slot in range(positions):
        which, index, hits, length = 0, 0, 0, 0
        for row in range(requests):
            for column in range(columns_of):
                hit = (page_table[row * columns_of + column] == slot).astype(jnp.int32)
                hits += hit
                which += hit * row
                index += hit * column
                length += hit * lengths[row]
        request_of.append(jnp.minimum(which, requests - 1))
        used.append(hits)
        live.append(jnp.clip(length - index * page_len, 0, page_len) * (hits > 0).astype(jnp.int32))

    def at_slot(values, slot):
        picked = values[0]
        for place in range(1, positions):
            picked = jnp.where(slot == place, values[place], picked)
        return picked

    row_ids = lax.broadcasted_iota(jnp.int32, (rows, 1), 0)
    row_head = lax.rem(row_ids, heads) // group
    row_step = row_ids // heads

    columns = new_rows.shape[2]
    column_ids = lax.broadcasted_iota(jnp.int32, (1, columns), 1)
    new_mask = (
        (lax.rem(column_ids, 2 * kv_local) == row_head)
        & (column_ids // (2 * kv_local) <= row_step)
    )
    for mine in range(owned):
        for layer in range(layers):
            new = new_rows[mine, layer]
            scores = scores_of(rows_of(queries[mine, layer]), new)
            peak, weights, total = softmax_parts(scores, new_mask)
            wide = new.astype(jnp.float32)
            values = jnp.concatenate([wide[kv_local:], wide[:kv_local]], axis=0)
            new_out[mine, layer] = jnp.dot(
                weights, values.astype(jnp.bfloat16), preferred_element_type=jnp.float32
            )
            new_peak[mine, layer] = jnp.broadcast_to(peak, (rows, head))
            new_sum[mine, layer] = jnp.broadcast_to(total, (rows, head))

    own_queries.wait()
    for copy in query_copies:
        copy.wait()
    for copy in own_pages:
        copy.wait()

    token_ids = lax.broadcasted_iota(jnp.int32, (1, page_len), 1)

    def attend(slot):
        query_rows = rows_of(layer_queries[at_slot(request_of, slot)])
        scores = scores_of(query_rows, pages[0][slot])
        for place in range(1, kv_local):
            scores = jnp.where(
                row_head == place, scores_of(query_rows, pages[place][slot]), scores
            )
        peak, weights, total = softmax_parts(scores, token_ids < at_slot(live, slot))
        out = jnp.dot(weights, pages[kv_local][slot], preferred_element_type=jnp.float32)
        for place in range(1, kv_local):
            out = jnp.where(
                row_head == place,
                jnp.dot(weights, pages[kv_local + place][slot], preferred_element_type=jnp.float32),
                out,
            )
        page_out[slot] = out
        page_peak[slot] = jnp.broadcast_to(peak, (rows, head))
        page_sum[slot] = jnp.broadcast_to(total, (rows, head))

    def page_for(key):
        slot, keep = 0, 0
        for q in range(positions):
            hit = (keys[q] == key).astype(jnp.int32)
            slot += hit * q
            keep += hit * used[q]
        return jnp.minimum(slot, positions - 1), keep

    halves = batches // 2
    passed = [key for key in range(halves, halves + quarter)] if by_key else []
    straight = [key for key in range(1, batches) if key not in passed] if by_key else []
    sources = [page_for(key) for key in range(batches)] if by_key else []
    straight_copies = [[] for _ in chunks]
    first_copies = [[] for _ in chunks]
    second_copies = [[] for _ in chunks]

    def send(chunk, entry, place):
        for key in passed + straight + [0]:
            slot, keep = sources[key]
            page = pages[chunk][slot]
            page = lax.select(keep > 0, page, jnp.zeros_like(page))
            if key == 0:
                landing[chunk][0] = page
                continue
            leaving[key, chunk] = page
            if key in passed:
                turn = key - halves
                copy = pltpu.make_async_remote_copy(
                    src_ref=leaving.at[key, chunk],
                    dst_ref=passing.at[turn, chunk],
                    send_sem=pass_send.at[turn, chunk],
                    recv_sem=pass_recv.at[turn, chunk],
                    device_id={"batch": down if turn % 2 else up},
                    device_id_type=MESH,
                )
                first_copies[chunk].append(copy)
            else:
                copy = pltpu.make_async_remote_copy(
                    src_ref=leaving.at[key, chunk],
                    dst_ref=landing[chunk].at[key],
                    send_sem=key_send.at[key, chunk],
                    recv_sem=key_recv.at[key, chunk],
                    device_id={"batch": exclusive_or(batch, key, batches)},
                    device_id_type=MESH,
                )
                straight_copies[chunk].append(copy)
            copy.start()

    def pass_on(chunk):
        for turn, first in enumerate(first_copies[chunk]):
            first.wait_recv()
            onward = exclusive_or(down if turn % 2 else up, turn, batches)
            copy = pltpu.make_async_remote_copy(
                src_ref=passing.at[turn, chunk],
                dst_ref=landing[chunk].at[halves + turn],
                send_sem=on_send.at[turn, chunk],
                recv_sem=key_recv.at[halves + turn, chunk],
                device_id={"batch": onward},
                device_id_type=MESH,
            )
            copy.start()
            second_copies[chunk].append(copy)

    for chunk, (entry, place) in enumerate(chunks):
        for copy in page_copies[chunk]:
            copy.wait_recv()
        if by_key:
            send(chunk, entry, place)
        if chunk < local_pages:
            attend(tensor * local_pages + chunk)
        if by_key and chunk > 0:
            pass_on(chunk - 1)
    for page in range(len(chunks), local_pages):
        attend(tensor * local_pages + page)
    for page in range(local_pages):
        for ahead in range(1, tensors):
            attend(lax.rem(tensor + tensors - ahead, tensors) * local_pages + page)

    lane = lax.broadcasted_iota(jnp.int32, (rows, head), 1)

    def merge(request):
        takes = [
            (request_of[slot] == request) & (used[slot] > 0) for slot in range(positions)
        ]
        top = jnp.full((rows, head), MASKED, jnp.float32)
        for slot in range(positions):
            top = jnp.maximum(top, jnp.where(takes[slot], page_peak[slot], MASKED))
        numerator = jnp.zeros((rows, head), jnp.float32)
        denominator = jnp.zeros((rows, head), jnp.float32)
        for slot in range(positions):
            factor = jnp.where(takes[slot], jnp.exp(page_peak[slot] - top), 0.0)
            numerator += factor * page_out[slot]
            denominator += factor * page_sum[slot]
        return numerator, jnp.where(lane < head // 2, top, denominator)

    part_copies = []
    for ahead in range(1, sections):
        other = lax.rem(section + ahead, sections)
        for mine in range(owned):
            numerator, stats = merge(other * owned + mine)
            outgoing[ahead - 1, mine, 0] = numerator
            outgoing[ahead - 1, mine, 1] = stats
        copy = pltpu.make_async_remote_copy(
            src_ref=outgoing.at[ahead - 1],
            dst_ref=merged.at[section],
            send_sem=part_sems.at[0, ahead - 1],
            recv_sem=part_sems.at[1, ahead - 1],
            device_id={"section": other},
            device_id_type=MESH,
        )
        copy.start()
        part_copies.append(copy)
    for mine in range(owned):
        numerator, stats = merge(section * owned + mine)
        merged[section, mine, 0] = numerator
        merged[section, mine, 1] = stats

    if by_key:
        pass_on(len(chunks) - 1)
    else:
        for slot in range(positions):
            for chunk, (entry, place) in enumerate(chunks):
                page = pages[chunk][slot]
                slots_out[slot][entry, place] = lax.select(
                    used[slot] > 0, page, jnp.zeros_like(page)
                )

    for copy in part_copies:
        copy.wait()
    for mine in range(owned):
        for layer in range(layers):
            numerator, stats = merged[layer, mine, 0], merged[layer, mine, 1]
            top, denominator = stats[:, :1], stats[:, head // 2 : head // 2 + 1]
            latest = new_peak[mine, layer]
            joint = jnp.maximum(top, latest)
            old_scale, new_scale = jnp.exp(top - joint), jnp.exp(latest - joint)
            result = (old_scale * numerator + new_scale * new_out[mine, layer]) / (
                old_scale * denominator + new_scale * new_sum[mine, layer]
            )
            attended[mine, layer] = result.reshape(steps, heads, head).astype(jnp.bfloat16)
    for chunk, (entry, place) in enumerate(chunks):
        if by_key:
            for copy in straight_copies[chunk] + second_copies[chunk]:
                copy.wait_recv()
            for slot in range(positions):
                slots_out[0][slot, entry, place] = landing[chunk][
                    jnp.minimum(keys[slot], batches - 1)
                ]
    for chunk in range(len(chunks)):
        for copy in (
            page_copies[chunk] + straight_copies[chunk] + first_copies[chunk]
            + second_copies[chunk]
        ):
            copy.wait_send()


def attend_and_order(prefill_cache, lengths, page_table, holder, queries, new_kv, by_key):
    tensors, sections = lax.axis_size("tensor"), lax.axis_size("section")
    batches, positions = holder.shape
    local_pages, cache_heads, page_len, head = (
        prefill_cache.shape[1],
        prefill_cache.shape[3],
        prefill_cache.shape[4],
        prefill_cache.shape[5],
    )
    kv_local = cache_heads // tensors
    owned, layers, steps, heads = queries.shape[:4]
    rows = steps * heads
    new_rows = new_kv.reshape(owned, layers, steps * 2 * kv_local, head)
    page = jax.ShapeDtypeStruct((2, kv_local, page_len, head), jnp.bfloat16)
    smem = pl.BlockSpec(memory_space=pltpu.SMEM)
    vmem = pl.BlockSpec(memory_space=pltpu.VMEM)

    def wide(*lead):
        return pltpu.VMEM(lead + (rows, head), jnp.float32)

    if by_key:
        outs = [jax.ShapeDtypeStruct((positions,) + page.shape, page.dtype)]
        turns = batches // 4
        key_scratch = [
            pltpu.VMEM((batches, 2 * kv_local, page_len, head), jnp.bfloat16),
            pltpu.VMEM((turns, 2 * kv_local, page_len, head), jnp.bfloat16),
            pltpu.SemaphoreType.DMA((batches, 2 * kv_local)),
            pltpu.SemaphoreType.DMA((batches, 2 * kv_local)),
            pltpu.SemaphoreType.DMA((turns, 2 * kv_local)),
            pltpu.SemaphoreType.DMA((turns, 2 * kv_local)),
            pltpu.SemaphoreType.DMA((turns, 2 * kv_local)),
            *[pltpu.VMEM((batches, page_len, head), jnp.bfloat16)] * (2 * kv_local),
        ]
    else:
        outs, key_scratch = [page] * positions, []
    result = pl.pallas_call(
        functools.partial(kernel, tensors, sections, batches, by_key),
        out_shape=outs + [jax.ShapeDtypeStruct(queries.shape, jnp.bfloat16)],
        in_specs=[smem, smem, smem, pl.BlockSpec(memory_space=pl.ANY), vmem, vmem],
        out_specs=[vmem] * (len(outs) + 1),
        scratch_shapes=[
            *[pltpu.VMEM((positions, page_len, head), jnp.bfloat16)] * (2 * kv_local),
            pltpu.VMEM((owned * sections, steps, heads, head), jnp.bfloat16),
            wide(positions), wide(positions), wide(positions),
            wide(owned, layers), wide(owned, layers), wide(owned, layers),
            wide(max(sections - 1, 1), owned, 2),
            wide(sections, owned, 2),
            pltpu.SemaphoreType.DMA((1 + 2 * kv_local,)),
            pltpu.SemaphoreType.DMA((max(tensors - 1, 1), local_pages, 2 * kv_local)),
            pltpu.SemaphoreType.DMA((max(tensors - 1, 1), local_pages, 2 * kv_local)),
            pltpu.SemaphoreType.DMA((2, max(sections - 1, 1))),
            pltpu.SemaphoreType.DMA((2, max(sections - 1, 1))),
        ] + key_scratch,
        compiler_params=pltpu.CompilerParams(collective_id=0, has_side_effects=True),
        name="attend_and_order",
    )(lengths, page_table.reshape(-1), holder[0], prefill_cache, queries, new_rows)
    return result[:-1], result[-1]


def on_device(prefill_cache, lengths, page_table, holder, queries, new_kv):
    batch_count, positions = holder.shape
    route_keys = holder[0]
    by_key = sends_by_key(batch_count, positions)
    pages, attended = attend_and_order(
        prefill_cache, lengths, page_table, holder, queries, new_kv, by_key
    )
    if by_key:
        decode_slots = pages[0]
    else:
        moving = (jnp.stack(pages),)
        for bit in range(lax.axis_size("batch").bit_length() - 1):
            take = route_keys // (1 << bit) % 2 == 1
            partner = jax.tree.map(
                lambda part, own: part.astype(own.dtype),
                partner_2(shortened(moving), "batch", bit),
                moving,
            )
            moving = pick_where(take, partner, moving)
        decode_slots = moving[0]
    return (attended, decode_slots.reshape((1,) + decode_slots.shape))


def solution(mesh):
    placed = (
        P("section", ("batch", "tensor"), None, None, None, None),
        P("batch"),
        P("batch", None),
        P(),
        P(("batch", "section"), None, None, "tensor", None),
        P(("batch", "section"), None, None, None, "tensor", None),
    )
    return jax.shard_map(
        on_device,
        mesh=mesh,
        in_specs=placed,
        out_specs=(
            P(("batch", "section"), None, None, "tensor", None),
            P("section", "batch", None, "tensor", None, None),
        ),
        check_vma=False,
    )
```

profile of v0, /device:TPU:0, one launch (start us, length us, event | category | flops | bytes accessed | tf_op | source)
XLA Modules:
  0.0 64.7 jit_solution(6384346540583465796)
XLA Ops:
  0.6 0.0 copy-start
  0.6 0.7 %copy-done = s32[8,4]{0,1:T(4,128)S(1)} copy-done((s32[8,4]{0,1:T(4,128)S(1)}, s32[8,4]{0,1:T(4,128)}, u32[]{:S(2)}) %copy-start) | copy-done | bytes 152
  1.3 0.6 slice_reduce_fusion.keys
  1.9 59.0 %attend_and_order.1 = (bf16[4,2,2,256,128]{4,3,2,1,0:T(8,128)(2,1)}, bf16[2,2,4,16,128]{4,3,2,1,0:T(8,128)(2,1)}) custom-call(s32[4]{0:T(128)} %lengths.1, s32[4]{0:T(128)} %bitcast.5, s32[4]{0:T(128)} %slice_reduce_fusion.keys, bf16[1,2,2,4,256,128]{5,4,3,2,1,0:T(8,128)(2,1)} %cache.1, bf16[2,2,4,16,128]{4,3,2,1,0:T(8,128)(2,1)} %queries.1, ...), custom_call_target="tpu_custom_call" | custom-call | tf_op jit(solution)/shard_map/attend_and_order/pallas_call | solution.py:423
  60.9 1.5 %copy.10 = bf16[2,2,4,16,128]{4,3,2,1,0:T(8,128)(2,1)} copy(bf16[2,2,4,16,128]{4,3,2,1,0:T(8,128)(2,1)} %get-tuple-element.8) | data formatting | bytes 131072
  62.4 2.3 %copy.11 = bf16[1,4,2,2,256,128]{5,4,3,2,1,0:T(8,128)(2,1)} copy(bf16[1,4,2,2,256,128]{5,4,3,2,1,0:T(8,128)(2,1)} %bitcast.3) | data formatting | bytes 2097152
Async XLA Ops:
  0.6 0.7 %copy-start = (s32[8,4]{0,1:T(4,128)S(1)}, s32[8,4]{0,1:T(4,128)}, u32[]{:S(2)}) copy-start(s32[8,4]{0,1:T(4,128)} %param.9) | copy-start | bytes 388
where the time goes:
time: 64.9 us; the launch traced here: 64.7 us
  Pallas kernels  59 us (91%)
  local copies, waits for them, and re-layouts  5.07 us (8%)
  between operations  0.65 us (1%)
    pallas_call x1, Pallas kernels, attend_and_order(): pl.pallas_call(functools.partial(kernel, tensors, sections, batches, by_k...  59 us
    unnamed x4, local copies, waits for them, and re-layouts  4.44 us

commit v1 on v0

--- a/solution.py
+++ b/solution.py
@@ -66,11 +66,12 @@
 
 
 def kernel(
-    tensors, sections, batches, by_key,
+    tensors, sections, batches, sent_keys,
     lengths, page_table, keys, cache, queries, new_rows,
     *rest,
 ):
     positions = keys.shape[0]
+    by_key = sent_keys is not None
     outs = 1 if by_key else positions
     slots_out = rest[:outs]
     attended, rest = rest[outs], rest[outs + 1 :]
@@ -80,8 +81,8 @@
     (layer_queries, page_out, page_peak, page_sum, new_out, new_peak, new_sum,
      outgoing, merged, load_sem, page_send, page_recv, query_sems, part_sems) = rest[:14]
     if by_key:
-        leaving, passing, key_send, key_recv, pass_send, pass_recv, on_send = rest[14:21]
-        landing = rest[21:]
+        leaving, key_send, key_recv = rest[14:17]
+        landing = rest[17:]
     tensor, section = lax.axis_index("tensor"), lax.axis_index("section")
     batch = lax.axis_index("batch")
     local_pages = cache.shape[1]
@@ -91,11 +92,6 @@
     columns_of = page_table.shape[0] // requests
     group = heads // kv_local
     rows = steps * heads
-
-    quarter = max(batches // 4, 1)
-    stretch, offset = batch // quarter, lax.rem(batch, quarter)
-    up = lax.rem(stretch + 1, 4) * quarter + offset
-    down = lax.rem(stretch + 3, 4) * quarter + offset
 
     barrier = pltpu.get_barrier_semaphore()
     greeted = 0
@@ -108,7 +104,7 @@
         pl.semaphore_signal(barrier, inc=1, device_id={"section": other}, device_id_type=MESH)
         greeted += 1
     if by_key:
-        for key in range(1, batches):
+        for key in sent_keys:
             other = exclusive_or(batch, key, batches)
             pl.semaphore_signal(barrier, inc=1, device_id={"batch": other}, device_id_type=MESH)
             greeted += 1
@@ -237,70 +233,35 @@
             keep += hit * used[q]
         return jnp.minimum(slot, positions - 1), keep
 
-    halves = batches // 2
-    passed = [key for key in range(halves, halves + quarter)] if by_key else []
-    straight = [key for key in range(1, batches) if key not in passed] if by_key else []
-    sources = [page_for(key) for key in range(batches)] if by_key else []
-    straight_copies = [[] for _ in chunks]
-    first_copies = [[] for _ in chunks]
-    second_copies = [[] for _ in chunks]
-
-    def send(chunk, entry, place):
-        for key in passed + straight + [0]:
-            slot, keep = sources[key]
+    key_copies = [[] for _ in chunks]
+
+    def send(chunk):
+        for key in sent_keys + (0,):
+            slot, keep = page_for(key)
             page = pages[chunk][slot]
             page = lax.select(keep > 0, page, jnp.zeros_like(page))
             if key == 0:
                 landing[chunk][0] = page
                 continue
             leaving[key, chunk] = page
-            if key in passed:
-                turn = key - halves
-                copy = pltpu.make_async_remote_copy(
-                    src_ref=leaving.at[key, chunk],
-                    dst_ref=passing.at[turn, chunk],
-                    send_sem=pass_send.at[turn, chunk],
-                    recv_sem=pass_recv.at[turn, chunk],
-                    device_id={"batch": down if turn % 2 else up},
-                    device_id_type=MESH,
-                )
-                first_copies[chunk].append(copy)
-            else:
-                copy = pltpu.make_async_remote_copy(
-                    src_ref=leaving.at[key, chunk],
-                    dst_ref=landing[chunk].at[key],
-                    send_sem=key_send.at[key, chunk],
-                    recv_sem=key_recv.at[key, chunk],
-                    device_id={"batch": exclusive_or(batch, key, batches)},
-                    device_id_type=MESH,
-                )
-                straight_copies[chunk].append(copy)
+            copy = pltpu.make_async_remote_copy(
+                src_ref=leaving.at[key, chunk],
+                dst_ref=landing[chunk].at[key],
+                send_sem=key_send.at[key, chunk],
+                recv_sem=key_recv.at[key, chunk],
+                device_id={"batch": exclusive_or(batch, key, batches)},
+                device_id_type=MESH,
+            )
             copy.start()
-
-    def pass_on(chunk):
-        for turn, first in enumerate(first_copies[chunk]):
-            first.wait_recv()
-            onward = exclusive_or(down if turn % 2 else up, turn, batches)
-            copy = pltpu.make_async_remote_copy(
-                src_ref=passing.at[turn, chunk],
-                dst_ref=landing[chunk].at[halves + turn],
-                send_sem=on_send.at[turn, chunk],
-                recv_sem=key_recv.at[halves + turn, chunk],
-                device_id={"batch": onward},
-                device_id_type=MESH,
-            )
-            copy.start()
-            second_copies[chunk].append(copy)
+            key_copies[chunk].append(copy)
 
     for chunk, (entry, place) in enumerate(chunks):
         for copy in page_copies[chunk]:
             copy.wait_recv()
         if by_key:
-            send(chunk, entry, place)
+            send(chunk)
         if chunk < local_pages:
             attend(tensor * local_pages + chunk)
-        if by_key and chunk > 0:
-            pass_on(chunk - 1)
     for page in range(len(chunks), local_pages):
         attend(tensor * local_pages + page)
     for page in range(local_pages):
@@ -346,9 +307,7 @@
         merged[section, mine, 0] = numerator
         merged[section, mine, 1] = stats
 
-    if by_key:
-        pass_on(len(chunks) - 1)
-    else:
+    if not by_key:
         for slot in range(positions):
             for chunk, (entry, place) in enumerate(chunks):
                 page = pages[chunk][slot]
@@ -371,21 +330,18 @@
             attended[mine, layer] = result.reshape(steps, heads, head).astype(jnp.bfloat16)
     for chunk, (entry, place) in enumerate(chunks):
         if by_key:
-            for copy in straight_copies[chunk] + second_copies[chunk]:
+            for copy in key_copies[chunk]:
                 copy.wait_recv()
             for slot in range(positions):
                 slots_out[0][slot, entry, place] = landing[chunk][
                     jnp.minimum(keys[slot], batches - 1)
                 ]
     for chunk in range(len(chunks)):
-        for copy in (
-            page_copies[chunk] + straight_copies[chunk] + first_copies[chunk]
-            + second_copies[chunk]
-        ):
+        for copy in page_copies[chunk] + key_copies[chunk]:
             copy.wait_send()
 
 
-def attend_and_order(prefill_cache, lengths, page_table, holder, queries, new_kv, by_key):
+def attend_and_order(prefill_cache, lengths, page_table, holder, queries, new_kv, sent_keys, number):
     tensors, sections = lax.axis_size("tensor"), lax.axis_size("section")
     batches, positions = holder.shape
     local_pages, cache_heads, page_len, head = (
@@ -405,23 +361,18 @@
     def wide(*lead):
         return pltpu.VMEM(lead + (rows, head), jnp.float32)
 
-    if by_key:
+    if sent_keys is not None:
         outs = [jax.ShapeDtypeStruct((positions,) + page.shape, page.dtype)]
-        turns = batches // 4
         key_scratch = [
             pltpu.VMEM((batches, 2 * kv_local, page_len, head), jnp.bfloat16),
-            pltpu.VMEM((turns, 2 * kv_local, page_len, head), jnp.bfloat16),
             pltpu.SemaphoreType.DMA((batches, 2 * kv_local)),
             pltpu.SemaphoreType.DMA((batches, 2 * kv_local)),
-            pltpu.SemaphoreType.DMA((turns, 2 * kv_local)),
-            pltpu.SemaphoreType.DMA((turns, 2 * kv_local)),
-            pltpu.SemaphoreType.DMA((turns, 2 * kv_local)),
             *[pltpu.VMEM((batches, page_len, head), jnp.bfloat16)] * (2 * kv_local),
         ]
     else:
         outs, key_scratch = [page] * positions, []
     result = pl.pallas_call(
-        functools.partial(kernel, tensors, sections, batches, by_key),
+        functools.partial(kernel, tensors, sections, batches, sent_keys),
         out_shape=outs + [jax.ShapeDtypeStruct(queries.shape, jnp.bfloat16)],
         in_specs=[smem, smem, smem, pl.BlockSpec(memory_space=pl.ANY), vmem, vmem],
         out_specs=[vmem] * (len(outs) + 1),
@@ -438,8 +389,8 @@
             pltpu.SemaphoreType.DMA((2, max(sections - 1, 1))),
             pltpu.SemaphoreType.DMA((2, max(sections - 1, 1))),
         ] + key_scratch,
-        compiler_params=pltpu.CompilerParams(collective_id=0, has_side_effects=True),
-        name="attend_and_order",
+        compiler_params=pltpu.CompilerParams(collective_id=number, has_side_effects=True),
+        name=f"attend_and_order_{number}",
     )(lengths, page_table.reshape(-1), holder[0], prefill_cache, queries, new_rows)
     return result[:-1], result[-1]
 
@@ -448,12 +399,23 @@
     batch_count, positions = holder.shape
     route_keys = holder[0]
     by_key = sends_by_key(batch_count, positions)
-    pages, attended = attend_and_order(
-        prefill_cache, lengths, page_table, holder, queries, new_kv, by_key
-    )
+    arrays = (prefill_cache, lengths, page_table, holder, queries, new_kv)
     if by_key:
-        decode_slots = pages[0]
+        half = batch_count // 2
+        far = tuple(range(half, half + batch_count // 4))
+        chosen = jnp.zeros((), jnp.int32)
+        branches = []
+        for place, key in enumerate(far):
+            chosen += jnp.any(route_keys == key).astype(jnp.int32) * (1 << place)
+        for number in range(1 << len(far)):
+            left_out = [key for place, key in enumerate(far) if not number >> place & 1]
+            sent = tuple(key for key in range(1, batch_count) if key not in left_out)
+            branches.append(
+                lambda *given, sent=sent, number=number: attend_and_order(*given, sent, number)
+            )
+        (decode_slots,), attended = lax.switch(chosen, branches, *arrays)
     else:
+        pages, attended = attend_and_order(*arrays, None, 0)
         moving = (jnp.stack(pages),)
         for bit in range(lax.axis_size("batch").bit_length() - 1):
             take = route_keys // (1 << bit) % 2 == 1

time: 64.9 us -> 63.4 us (0.977)
  Pallas kernels: 59 us -> 56.8 us
  local copies, waits for them, and re-layouts: 5.07 us -> 2.97 us
  other arithmetic: 0 us -> 1.33 us
  between operations: 0.65 us -> 1.98 us
    unnamed x4 -> x8, local copies, waits for them, and re-layouts: 4.44 us -> 2.26 us
    pallas_call x1, Pallas kernels: 59 us -> 56.8 us  [attend_and_order(): pl.pallas_call(functools.partial(kernel, tensors, sections, batches, sent...]
    reduce_or x0 -> x1, other arithmetic: none -> 1.33 us  [on_device(): chosen += jnp.any(route_keys == key).astype(jnp.int32) * (1 << place)]
where the time goes in v1:
time: 63.4 us; the launch traced here: 63.1 us
  Pallas kernels  56.8 us (90%)
  local copies, waits for them, and re-layouts  2.97 us (5%)
  between operations  1.98 us (3%)
  other arithmetic  1.33 us (2%)
    pallas_call x1, Pallas kernels, attend_and_order(): pl.pallas_call(functools.partial(kernel, tensors, sections, batches, sent...  56.8 us
    unnamed x8, local copies, waits for them, and re-layouts  2.26 us
    reduce_or x1, other arithmetic, on_device(): chosen += jnp.any(route_keys == key).astype(jnp.int32) * (1 << place)  1.33 us

profile of v1, /device:TPU:0, one launch (start us, length us, event | category | flops | bytes accessed | tf_op | source)
XLA Modules:
  0.0 63.1 jit_solution(18383240008290627581)
XLA Ops:
  0.6 1.3 %compare_reduce_fusion = (pred[]{:T(512)}, pred[]{:T(512)}) fusion(s32[8,4]{0,1:T(4,128)} %param.13), kind=kLoop, calls=%fused_computation.4 | loop fusion | flops 14 | bytes 18 | tf_op jit(solution)/shard_map/reduce_or | solution.py:409
  2.6 0.0 copy-start.4
  3.3 0.0 copy-start.5
  3.3 0.0 copy-start.6
  3.3 0.0 copy-done.4
  3.3 0.6 copy-done.5
  3.9 0.0 copy-done.6
  4.0 57.5 %conditional.1 = (bf16[2,2,4,16,128]{4,3,2,1,0:T(8,128)(2,1)S(1)}, bf16[1,4,2,2,256,128]{5,4,3,2,1,0:T(8,128)(2,1)S(1)}) conditional(s32[]{:T(128)} %clamp.3, (s32[4,1]{0,1:T(1,128)S(1)}, s32[8,4]{0,1:T(4,128)S(1)}, bf16[2,2,4,2,2,128]{5,4,3,2,1,0:T(2,128)(2,1)}, s32[4]{0:T(128)S(1)}, ...), branch_computations={%region_2.0_spmd, %region_3.0_spmd, %region_4.0_spmd, %region_5.0_... | conditional | bytes 65868 | solution.py:416
  4.0 0.0 copy-start.3
  4.0 0.1 copy.15
  4.0 0.5 slice_bitcast_fusion.3.keys
  4.6 0.1 copy-done.3
  4.7 56.8 %attend_and_order_3.1 = (bf16[4,2,2,256,128]{4,3,2,1,0:T(8,128)(2,1)S(1)}, bf16[2,2,4,16,128]{4,3,2,1,0:T(8,128)(2,1)S(1)}) custom-call(s32[4]{0:T(128)S(1)} %get-tuple-element.81.lengths, s32[4]{0:T(128)S(1)} %bitcast.31, s32[4]{0:T(128)} %slice_bitcast_fusion.3.keys, bf16[1,2,2,4,256,128]{5,4,3,2,1,0:T(8,128)(2,1)} %get-tuple-element.84.cache, ...), custom_call_target="tpu_custom_call" | custom-call | tf_op jit(solution)/shard_map/cond/branch_3_fun/attend_and_order_3/pallas_call | solution.py:374
  61.5 0.6 %copy.26 = bf16[2,2,4,16,128]{4,3,2,1,0:T(8,128)(2,1)} copy(bf16[2,2,4,16,128]{4,3,2,1,0:T(8,128)(2,1)S(1)} %get-tuple-element.128) | data formatting | bytes 131072
  62.1 1.0 %copy.27 = bf16[1,4,2,2,256,128]{5,4,3,2,1,0:T(8,128)(2,1)} copy(bf16[1,4,2,2,256,128]{5,4,3,2,1,0:T(8,128)(2,1)S(1)} %get-tuple-element.129) | data formatting | bytes 2097152
Async XLA Ops:
  2.6 0.7 %copy-start.4 = (s32[8,4]{0,1:T(4,128)S(1)}, s32[8,4]{0,1:T(4,128)}, u32[]{:S(2)}) copy-start(s32[8,4]{0,1:T(4,128)} %param.13) | copy-start | bytes 388
  3.3 0.7 %copy-start.5 = (s32[4,1]{0,1:T(1,128)S(1)}, s32[4,1]{0,1:T(1,128)}, u32[]{:S(2)}) copy-start(s32[4,1]{0,1:T(1,128)} %param.12) | copy-start | bytes 52
  3.3 0.7 %copy-start.6 = (s32[4]{0:T(128)S(1)}, s32[4]{0:T(128)}, u32[]{:S(2)}) copy-start(s32[4]{0:T(128)} %param.11) | copy-start | bytes 52
  4.0 0.7 %copy-start.3 = (bf16[2,2,4,2,2,128]{5,4,3,2,1,0:T(2,128)(2,1)S(1)}, bf16[2,2,4,2,2,128]{5,4,3,2,1,0:T(2,128)(2,1)}, u32[]{:S(2)}) copy-start(bf16[2,2,4,2,2,128]{5,4,3,2,1,0:T(2,128)(2,1)} %get-tuple-element.86) | copy-start | bytes 49156 | tf_op jit(solution)/shard_map/cond
